TPU v7x, 32 devices: a whole 2x2x4 slice. The times are simulated.
32 devices in a mesh: dp: 4 (over x, core), fsdp: 8 (over z, y).
Axes of the slice: x: 2, y: 2, z: 4, core: 2. Of those that a mesh axis runs over, the one named last changes fastest.
Arguments:
- queries: bfloat16 [64, 128, 1280], P(('dp', 'fsdp')), may hold values from -100 to 100
- keys: bfloat16 [64, 128, 1280], P(('dp', 'fsdp')), may hold values from -100 to 100
- values: bfloat16 [64, 128, 1280], P(('dp', 'fsdp')), may hold values from -64 to 64
- block_len: int32 [64], P(('dp', 'fsdp')), may hold values from 0 to 128, as said below
- target: int32 [64], P(('dp', 'fsdp')), may hold values from 0 to 2, as said below
- cotangent: bfloat16 [32, 128, 1280], P(('dp', 'fsdp')), may hold values from -6 to 6
- out_weight: bfloat16 [1280, 1280], P('fsdp'), may hold values from -0.15625 to 0.15625
Outputs:
- embedding: bfloat16 [32, 128, 1280], P(('dp', 'fsdp'))
- weight_grad: float32 [1280, 1280], P('fsdp')
Inputs may be any that keep to these rules, and one draw needn't show every extreme that they name: `block_len`: 0 exactly in the empty slots, those with target 2; live blocks hold 1 to 128 patches; in every draw some device has all its slots live and full. `target`: t < 1: output slot t of the same device; 1 <= t < 2: output slot t - 1 of the next device along dp (wrapping), same fsdp index; t = 2: empty slot; live values are distinct within a device, every output slot receives exactly one block, and in every draw some device has all 2 slots live.
All inputs are finite; a program needn't handle non-finite values.
Results may differ from a plain program's by a relative error of at most 0.012.
Values may be sent and summed in bfloat16 or wider, within the bound.
A program may use at most 64 MiB of HBM per device.

v0:
```python
import jax
import jax.numpy as jnp
from jax import lax
from jax.sharding import PartitionSpec as P

HEADS = 16


def from_behind(shard, axis, by):
    size = lax.axis_size(axis)
    return lax.ppermute(shard, axis, [(i, (i + by) % size) for i in range(size)])


def attend(query, key_block, value_block, length):
    blocks, window, features = query.shape
    head_dim = features // HEADS
    shape = (blocks, window, HEADS, head_dim)
    query_heads = query.reshape(shape)
    key_heads = key_block.reshape(shape)
    value_heads = value_block.reshape(shape)
    scores = jnp.einsum(
        "bqhd,bkhd->bhqk", query_heads, key_heads, preferred_element_type=jnp.float32
    ) * head_dim ** (-0.5)
    position = jnp.arange(window, dtype=jnp.int32)
    usable = position[None, :] < length[:, None]
    scores = jnp.where(usable[:, None, None, :], scores, -1e30)
    highest = jnp.max(scores, axis=-1, keepdims=True)
    exponent = jnp.exp(scores - highest)
    attn_weights = (exponent / jnp.sum(exponent, axis=-1, keepdims=True)).astype(jnp.bfloat16)
    mixed_out = jnp.einsum(
        "bhqk,bkhd->bqhd", attn_weights, value_heads, preferred_element_type=jnp.float32
    )
    mixed_out = jnp.where(usable[:, :, None, None], mixed_out, 0.0)
    return mixed_out.reshape(blocks, window, features).astype(jnp.bfloat16)


def pack_slots(target, arrays):
    slot_count = target.shape[0]
    select_map = (target[None, :] == jnp.arange(slot_count, dtype=jnp.int32)[:, None]).astype(
        jnp.bfloat16
    )
    return tuple(
        (
            jnp.einsum(
                "ts,swd->twd", select_map, array_item, preferred_element_type=jnp.float32
            ).astype(jnp.bfloat16)
            for array_item in arrays
        )
    )


def local(queries, keys, values, block_len, target, cotangent, out_weight):
    own_slots = cotangent.shape[0]
    local_out = attend(queries, keys, values, block_len)
    out_pack = pack_slots(target, (local_out,))[0]
    arrived = from_behind(out_pack[own_slots:], "dp", 1)
    attended = out_pack[:own_slots] + arrived
    features = attended.shape[-1]
    flat_rows = attended.reshape(-1, features)
    row_total = flat_rows.shape[0]
    columns = flat_rows
    projected = jnp.dot(
        columns,
        lax.all_gather(out_weight, "fsdp", axis=0, tiled=True),
        preferred_element_type=jnp.float32,
    )
    embedding = projected.astype(jnp.bfloat16).reshape(attended.shape)
    cot_rows = cotangent.reshape(row_total, features)
    columns = flat_rows
    fsdp_summed = lax.psum_scatter(
        lax.dot_general(
            columns, cot_rows, (((0,), (0,)), ((), ())), preferred_element_type=jnp.float32
        ).astype(jnp.bfloat16),
        "fsdp",
        scatter_dimension=0,
        tiled=True,
    ).astype(jnp.float32)
    summed = lax.psum(fsdp_summed, "dp")
    squares = lax.psum(jnp.sum(summed * summed), "fsdp")
    norm_value = jnp.sqrt(squares + 1e-06)
    factor = jnp.minimum(1.0, float(features) / norm_value)
    return (embedding, summed * factor)


def solution(mesh):
    placed = (
        P(("dp", "fsdp"), None, None),
        P(("dp", "fsdp"), None, None),
        P(("dp", "fsdp"), None, None),
        P(("dp", "fsdp")),
        P(("dp", "fsdp")),
        P(("dp", "fsdp"), None, None),
        P("fsdp", None),
    )
    return jax.shard_map(
        local,
        mesh=mesh,
        in_specs=placed,
        out_specs=(P(("dp", "fsdp"), None, None), P("fsdp", None)),
        check_vma=False,
    )
```

profile of v0, /device:TPU:0, one launch (start us, length us, event | category | flops | bytes accessed | tf_op | source)
XLA Modules:
  0.0 201.7 jit_solution(7435030648020174563)
XLA Ops:
  7.2 0.0 copy-start
  7.2 0.0 copy-start.1
  7.2 0.0 reduce-scatter.2.cloned.1.call-start
  7.2 0.8 iota_compare_fusion
  8.0 1.4 copy.19
  9.5 1.4 copy.20
  10.9 0.0 copy-done.1
  10.9 0.3 copy.21
  11.3 2.3 %fusion.18 = (f32[2,16,128]{2,1,0:T(8,128)S(1)}, f32[2,16,128,128]{2,3,1,0:T(8,128)}) fusion(pred[2,128]{1,0:T(4,128)(4,1)S(1)} %iota_compare_fusion, bf16[2,128,16,80]{1,3,2,0:T(8,128)(2,1)S(1)} %bitcast.25, bf16[2,128,16,80]{1,3,2,0:T(8,128)(2,1)S(1)} %bitcast.26), kind=kOutput, calls=%fused_computation.29 | convolution fusion | flops 85983360 | bytes 3424512 | tf_op jit(solution)/shard_map/sub | solution.py:28
  13.6 0.0 copy-start.2
  13.6 2.1 %fusion.3 = bf16[2,16,128,80]{2,3,1,0:T(8,128)(2,1)S(1)} fusion(bf16[2,128,16,80]{1,3,2,0:T(8,128)(2,1)S(1)} %bitcast.24, f32[2,16,128,128]{2,3,1,0:T(8,128)} %get-tuple-element.3, f32[2,16,128]{2,1,0:T(8,128)S(1)} %get-tuple-element.2, pred[2,128]{1,0:T(4,128)(4,1)S(1)} %iota_compare_fusion), kind=kOutput, calls=%fused_computation.10 | convolution fusion | flops 85590016 | bytes 3424512 | tf_op jit(solution)/shard_map/bhqk,bkhd->bqhd/dot_general | solution.py:30
  15.8 1.0 copy.23
  16.7 0.0 copy-done.2
  16.7 0.8 convolution_convert_fusion.1
  17.6 0.7 slice.9
  18.3 0.5 collective-permute-start
  18.9 6.7 %collective-permute-done = bf16[1,128,1280]{2,1,0:T(8,128)(2,1)S(1)} collective-permute-done((bf16[1,128,1280]{2,1,0:T(8,128)(2,1)S(1)}, bf16[1,128,1280]{2,1,0:T(8,128)(2,1)S(1)}, u32[]{:S(2)}, u32[]{:S(2)}) %collective-permute-start) | collective-permute-done | bytes 327712 | tf_op jit(solution)/shard_map/ppermute | solution.py:11
  25.6 0.8 slice_add_fusion
  26.3 0.0 copy-done
  26.3 2.8 %convolution_convert_fusion = bf16[1280,1280]{1,0:T(8,128)(2,1)} fusion(bf16[1,128,1280]{2,1,0:T(8,128)(2,1)S(1)} %copy-done, bf16[1,128,1280]{2,0,1:T(2,128)(2,1)S(1)} %slice_add_fusion), kind=kOutput, calls=%fused_computation.1 | convolution fusion | flops 421068800 | bytes 3932160 | tf_op jit(solution)/shard_map/dot_general | solution.py:71
  29.1 0.0 reduce-scatter.2.cloned.1.call-update
  29.1 0.0 all-gather.2.cloned.1.call-start
  29.2 0.7 all-gather.2.cloned.1.call-update
  29.9 77.8 %reduce-scatter.2.cloned.1.call-done = bf16[160,1280]{1,0:T(8,128)(2,1)} async-done(((bf16[1280,1280]{1,0:T(8,128)(2,1)}), bf16[160,1280]{1,0:T(8,128)(2,1)}) %reduce-scatter.2.cloned.1.call-update) | async-done | bytes 409616 | tf_op jit(solution)/shard_map/reduce_scatter | solution.py:70
  107.7 20.2 %all-reduce.1 = f32[160,1280]{1,0:T(8,128)S(1)} all-reduce(bf16[160,1280]{1,0:T(8,128)(2,1)} %reduce-scatter.2.cloned.1.call-done), channel_id=1, replica_groups=mesh['dp'=4,'fsdp'=8] {'dp'}, use_global_device_ids=true, to_apply=%region_3.4 | all-reduce | flops 204800 | bytes 1228800 | tf_op jit(solution)/shard_map/psum | solution.py:78
  127.9 0.8 multiply_reduce_fusion
  128.7 41.6 %all-gather.2.cloned.1.call-done = bf16[1280,1280]{1,0:T(8,128)(2,1)} async-done(((bf16[160,1280]{1,0:T(8,128)(2,1)}), bf16[1280,1280]{1,0:T(8,128)(2,1)}) %all-gather.2.cloned.1.call-update) | async-done | bytes 3276816 | tf_op jit(solution)/shard_map/all_gather | solution.py:64
  170.3 3.3 %fusion.1 = bf16[1,128,1280]{2,1,0:T(8,128)(2,1)} fusion(bf16[1280,1280]{1,0:T(8,128)(2,1)} %all-gather.2.cloned.1.call-done, bf16[1,128,1280]{2,0,1:T(2,128)(2,1)S(1)} %slice_add_fusion), kind=kOutput, calls=%fused_computation.4 | convolution fusion | flops 419594240 | bytes 3932160 | tf_op jit(solution)/shard_map/dot_general | solution.py:62
  173.5 19.7 %psum.15 = f32[]{:T(128)} all-reduce(f32[]{:T(128)} %multiply_reduce_fusion), channel_id=1, replica_groups=mesh['dp'=4,'fsdp'=8] {'fsdp'}, use_global_device_ids=true, to_apply=%region_5.6 | all-reduce | flops 1 | bytes 8 | tf_op jit(solution)/shard_map/psum | solution.py:79
  194.0 0.9 broadcast_multiply_fusion
  (1 shorter events, 0.0 us)
Async XLA Ops:
  7.2 19.2 %copy-start = (bf16[1,128,1280]{2,1,0:T(8,128)(2,1)S(1)}, bf16[1,128,1280]{2,1,0:T(8,128)(2,1)}, u32[]{:S(2)}) copy-start(bf16[1,128,1280]{2,1,0:T(8,128)(2,1)} %param.12) | copy-start | bytes 983044
  7.2 3.7 %copy-start.1 = (bf16[2,128,1280]{2,1,0:T(8,128)(2,1)S(1)}, bf16[2,128,1280]{2,1,0:T(8,128)(2,1)}, u32[]{:S(2)}) copy-start(bf16[2,128,1280]{2,1,0:T(8,128)(2,1)} %param.9) | copy-start | bytes 1966084
  7.2 100.5 %reduce-scatter.2.cloned.1.call-start = ((), (), s32[]{:S(2)}) async-start(), calls=%async_computation.2 | async-start | bytes 3686400 | tf_op jit(solution)/shard_map/reduce_scatter | solution.py:70
  13.6 3.1 %copy-start.2 = (s32[2]{0:T(128)S(1)}, s32[2]{0:T(128)}, u32[]{:S(2)}) copy-start(s32[2]{0:T(128)} %param.11) | copy-start | bytes 28
  18.3 7.2 %collective-permute-start = (bf16[1,128,1280]{2,1,0:T(8,128)(2,1)S(1)}, bf16[1,128,1280]{2,1,0:T(8,128)(2,1)S(1)}, u32[]{:S(2)}, u32[]{:S(2)}) collective-permute-start(bf16[1,128,1280]{2,1,0:T(8,128)(2,1)S(1)} %copy.24), channel_id=1, source_target_pairs={{0,8},{8,16},{16,24},{24,0},{1,9},{9,17},{17,25},{25,1},{2,10},{10... | collective-permute-start | bytes 983048 | tf_op jit(solution)/shard_map/ppermute | solution.py:11
  29.1 141.2 %all-gather.2.cloned.1.call-start = ((), (), s32[]{:S(2)}) async-start(), calls=%async_computation.1 | async-start | bytes 3686400 | tf_op jit(solution)/shard_map/all_gather | solution.py:64
Sparse Core Ops, SparseCore 0:
  29.2 78.3 reduce-scatter.1
  109.8 60.3 all-gather.1
where the time goes:
time: 202 us
  waiting for transfers between devices  127 us (63%)
  blocking collectives  40 us (20%)
  between operations  14.8 us (7%)
  matrix products  11.3 us (6%)
  local copies, waits for them, and re-layouts  4.93 us (2%)
  other arithmetic  3.32 us (2%)
    reduce_scatter x1, waiting for transfers between devices, local(): lax.psum_scatter(lax.dot_general(columns, cot_rows, (((0,), (0,)), ((), (...  77.8 us
    all_gather x1, waiting for transfers between devices, local(): lax.all_gather(out_weight, 'fsdp', axis=0, tiled=True)  41.6 us
    psum x1, blocking collectives, local(): summed = lax.psum(fsdp_summed, 'dp')  20.2 us
    psum x1, blocking collectives, local(): squares = lax.psum(jnp.sum(summed * summed), 'fsdp')  19.7 us
    ppermute x1, waiting for transfers between devices, from_behind(): lax.ppermute(shard, axis, [(i, (i + by) % size) for i in range(size)])  6.68 us
  transfers between devices with their start and end apart: 3, of which 3 were waited for; matrix products, arithmetic and copies ran while one was open for 0% of the time, Pallas kernels for 0%

commit v1 on v0

v1 whole, which is shorter than its diff:
```python
import functools
import math

import jax
import jax.numpy as jnp
from jax import lax
from jax.experimental import pallas as pl
from jax.experimental.pallas import tpu as pltpu
from jax.sharding import PartitionSpec as P

HEADS = 16
LANES = 128
MESH = pl.DeviceIdType.MESH
F32 = jnp.float32
BF16 = jnp.bfloat16


def starts_of(width, group):
    tiles = width // LANES
    window = -(-tiles // group) * LANES
    return window, [min(i * window, width - window) for i in range(group)]


def kernel(
    n_dp, n_fs, group, finish,
    len_ref, tgt_ref, q_ref, k_ref, v_ref, cot_ref, w_ref,
    emb_ref, grad_ref,
    wq, cq, mine, nxt, arr, placed, gpart, yrecv, zsend, zrecv, esend, ebuf, tbuf, sbuf, srecv,
    wz_s, wz_r, wy_s, wy_r, c_s, c_r, n_s, n_r, p_s, p_r, gy_s, gy_r, gz_s, gz_r,
    e_s, e_r, t_s, t_r, q_s, q_r,
):
    slots, rows, width = q_ref.shape
    shard = w_ref.shape[0]
    hd = width // HEADS
    window, starts = starts_of(width, group)
    over = group * window - width
    nz = n_fs // 2
    d, f = lax.axis_index("dp"), lax.axis_index("fsdp")
    base = (d // group) * group
    gi = d - base
    z, y = f // 2, f % 2
    other = z * 2 + (1 - y)
    ahead, behind = (d + 1) % n_dp, (d + n_dp - 1) % n_dp
    mates = [(gi + j) % group for j in range(1, group)]

    def start_of(i):
        if group == 1:
            return 0
        return pl.multiple_of(i * window - (i // (group - 1)) * over, LANES)

    def copy(src, dst, s, r, to):
        return pltpu.make_async_remote_copy(
            src_ref=src, dst_ref=dst, send_sem=s, recv_sem=r, device_id=to, device_id_type=MESH
        )

    barrier = pltpu.get_barrier_semaphore()
    peers = [(ahead, f), (behind, f)]
    peers += [(base + m, f) for m in mates]
    peers += [(d, (f + j) % n_fs) for j in range(1, n_fs)]
    for peer in peers:
        pl.semaphore_signal(barrier, inc=1, device_id=peer, device_id_type=MESH)
    pl.semaphore_wait(barrier, len(peers))

    my_cols = pl.ds(start_of(gi), window)
    my_rows = pl.ds(pl.multiple_of(gi * rows, rows), rows)

    def w_at(index):
        return wq.at[pl.ds(pl.multiple_of(index * shard, shard), shard), :]

    sends = []
    w_src = w_ref.at[:, my_cols]
    wz = []
    for j in range(1, nz):
        c = copy(w_src, w_at(f), wz_s.at[j], wz_r.at[j], (d, ((z + j) % nz) * 2 + y))
        c.start()
        wz.append(c)
    wy = [copy(w_src, w_at(f), wy_s.at[0], wy_r.at[0], (d, other))]
    wy[0].start()
    cots = []
    for j, m in enumerate(mates):
        c = copy(
            cot_ref.at[0, :, pl.ds(start_of(m), window)], cq.at[my_rows, :],
            c_s.at[j], c_r.at[j], (base + m, f),
        )
        c.start()
        cots.append(c)
    wq[pl.ds(pl.multiple_of(f * shard, shard), shard), :] = w_ref[:, my_cols]
    cq[my_rows, :] = cot_ref[0, :, my_cols]

    key_pos = lax.broadcasted_iota(jnp.int32, (rows, rows), 1)
    row_pos = lax.broadcasted_iota(jnp.int32, (rows, LANES), 0)
    lens = [len_ref[s] for s in range(slots)]
    usable = [key_pos < lens[s] for s in range(slots)]
    limit = [[jnp.where(tgt_ref[s] == t, lens[s], 0) for s in range(slots)] for t in range(2)]
    keep = [[row_pos < limit[t][s] for s in range(slots)] for t in range(2)]
    tiles = {}
    half = width // 2
    nexts = []

    def send_next(part):
        cols = pl.ds(part * half, half)
        c = copy(nxt.at[:, cols], arr.at[:, cols], n_s.at[part], n_r.at[part], (ahead, f))
        c.start()
        nexts.append(c)

    for h in range(HEADS):
        first, last = h * hd, (h + 1) * hd
        lo, hi = first // LANES * LANES, -(-last // LANES) * LANES
        lane = lax.broadcasted_iota(jnp.int32, (rows, hi - lo), 1) + lo
        inside = (lane >= first) & (lane < last)
        for s in range(slots):
            query = jnp.where(inside, q_ref[s, :, lo:hi].astype(F32), 0.0).astype(BF16)
            scores = lax.dot_general(
                query, k_ref[s, :, lo:hi], (((1,), (1,)), ((), ())), preferred_element_type=F32
            ) * hd ** (-0.5)
            scores = jnp.where(usable[s], scores, -1e30)
            exponent = jnp.exp(scores - jnp.max(scores, axis=-1, keepdims=True))
            weights = (exponent / jnp.sum(exponent, axis=-1, keepdims=True)).astype(BF16)
            mixed = jnp.dot(weights, v_ref[s, :, lo:hi], preferred_element_type=F32)
            mixed = jnp.where(inside, mixed, 0.0)
            for t in range(lo // LANES, hi // LANES):
                piece = mixed[:, t * LANES - lo:(t + 1) * LANES - lo]
                tiles[s, t] = tiles[s, t] + piece if (s, t) in tiles else piece
        for t in range(lo // LANES, hi // LANES):
            if (t + 1) * LANES <= last:
                cols = slice(t * LANES, (t + 1) * LANES)
                for dest, ref in ((0, mine), (1, nxt)):
                    total = sum(
                        jnp.where(keep[dest][s], tiles[s, t], 0.0) for s in range(slots)
                    )
                    ref[:, cols] = total.astype(BF16)
        if last == half:
            send_next(0)
    send_next(1)

    for j in range(1, nz):
        wz[j - 1].wait_recv()
        from_f = ((z + nz - j) % nz) * 2 + y
        c = copy(w_at(from_f), w_at(from_f), wy_s.at[j], wy_r.at[j], (d, other))
        c.start()
        wy.append(c)

    casts = []
    for part in range(2):
        nexts[part].wait_recv()
        cols = pl.ds(part * half, half)
        placed[my_rows, cols] = mine[:, cols] + arr[:, cols]
        for j, m in enumerate(mates):
            c = copy(
                placed.at[my_rows, cols], placed.at[my_rows, cols],
                p_s.at[part, j], p_r.at[part, j], (base + m, f),
            )
            c.start()
            casts.append(c)
    for c in cots + casts:
        c.wait_recv()

    step = 2 * LANES
    for i in range(width // step):
        gpart[i * step:(i + 1) * step, :] = lax.dot_general(
            placed[:, i * step:(i + 1) * step], cq[...], (((0,), (0,)), ((), ())),
            preferred_element_type=F32,
        ).astype(BF16)

    def g_rows(index):
        return pl.ds(pl.multiple_of(index * shard, shard), shard)

    order = list(range(1, nz)) + [0]
    gy = []
    for j in order:
        zj = (z + j) % nz
        c = copy(
            gpart.at[g_rows(zj * 2 + (1 - y)), :], yrecv.at[zj],
            gy_s.at[j], gy_r.at[j], (d, other),
        )
        c.start()
        gy.append(c)
    gz = []
    for j, c in zip(order, gy):
        zj = (z + j) % nz
        c.wait_recv()
        pair = gpart[g_rows(zj * 2 + y), :].astype(F32) + yrecv[zj].astype(F32)
        if j == 0:
            own = pair
        else:
            zsend[j] = pair.astype(BF16)
            c = copy(zsend.at[j], zrecv.at[j], gz_s.at[j], gz_r.at[j], (d, zj * 2 + y))
            c.start()
            gz.append(c)

    for c in wy:
        c.wait_recv()
    embs = []
    for i in range(group):
        esend[i] = jnp.dot(
            placed[i * rows:(i + 1) * rows, :], wq[...], preferred_element_type=F32
        ).astype(BF16)
    for j, m in enumerate(mates):
        c = copy(esend.at[m], ebuf.at[gi], e_s.at[j], e_r.at[j], (base + m, f))
        c.start()
        embs.append(c)
    ebuf[gi] = esend[gi]

    for c in gz:
        c.wait_recv()
    for j in range(1, nz):
        own = own + zrecv[j].astype(F32)
    tbuf[gi] = own.astype(BF16)
    turns = []
    for j, m in enumerate(mates):
        c = copy(tbuf.at[gi], tbuf.at[gi], t_s.at[j], t_r.at[j], (base + m, f))
        c.start()
        turns.append(c)
    for c in embs:
        c.wait_recv()
    ends = starts[1:] + [width]
    for i in range(group):
        emb_ref[0, :, starts[i]:ends[i]] = ebuf[i, :, 0:ends[i] - starts[i]]
    for c in turns:
        c.wait_recv()
    squares = []
    if finish:
        total = jnp.zeros((8, LANES), F32)
        for i in range(group):
            for col in range(0, ends[i] - starts[i], LANES):
                tile = tbuf[i, :, col:col + LANES].astype(F32)
                total = total + jnp.sum((tile * tile).reshape(shard // 8, 8, LANES), axis=0)
        sbuf[...] = total
        for j in range(1, n_fs):
            c = copy(sbuf, srecv.at[j], q_s.at[j], q_r.at[j], (d, (f + j) % n_fs))
            c.start()
            squares.append(c)
        for c in squares:
            c.wait_recv()
        for j in range(1, n_fs):
            total = total + srecv[j]
        norm = jnp.sqrt(jnp.sum(total, keepdims=True) + 1e-06)
        factor = jnp.minimum(1.0, float(width) / norm)
    for i in range(group):
        tile = tbuf[i, :, 0:ends[i] - starts[i]].astype(F32)
        grad_ref[:, starts[i]:ends[i]] = tile * factor if finish else tile
    for c in wz + wy + cots + nexts + casts + gy + gz + embs + turns + squares:
        c.wait_send()


def local(n_dp, n_fs, group, queries, keys, values, block_len, target, cotangent, out_weight):
    slots, rows, width = queries.shape
    shard = out_weight.shape[0]
    window, starts = starts_of(width, group)
    nz = n_fs // 2
    finish = group == n_dp
    vmem = pl.BlockSpec(memory_space=pltpu.VMEM)
    smem = pl.BlockSpec(memory_space=pltpu.SMEM)
    sem = lambda *shape: pltpu.SemaphoreType.DMA(shape)
    mates = max(group - 1, 1)
    embedding, grad = pl.pallas_call(
        functools.partial(kernel, n_dp, n_fs, group, finish),
        out_shape=(
            jax.ShapeDtypeStruct(cotangent.shape, BF16),
            jax.ShapeDtypeStruct((shard, width), F32),
        ),
        in_specs=[smem, smem] + [vmem] * 5,
        out_specs=(vmem, vmem),
        scratch_shapes=[
            pltpu.VMEM((width, window), BF16),
            pltpu.VMEM((group * rows, window), BF16),
            pltpu.VMEM((rows, width), BF16),
            pltpu.VMEM((rows, width), BF16),
            pltpu.VMEM((rows, width), BF16),
            pltpu.VMEM((group * rows, width), BF16),
            pltpu.VMEM((width, window), BF16),
            pltpu.VMEM((nz, shard, window), BF16),
            pltpu.VMEM((nz, shard, window), BF16),
            pltpu.VMEM((nz, shard, window), BF16),
            pltpu.VMEM((group, rows, window), BF16),
            pltpu.VMEM((group, rows, window), BF16),
            pltpu.VMEM((group, shard, window), BF16),
            pltpu.VMEM((8, LANES), F32),
            pltpu.VMEM((n_fs, 8, LANES), F32),
            sem(nz), sem(nz), sem(nz), sem(nz), sem(mates), sem(mates), sem(2), sem(2),
            sem(2, mates), sem(2, mates), sem(nz), sem(nz), sem(nz), sem(nz),
            sem(mates), sem(mates), sem(mates), sem(mates), sem(n_fs), sem(n_fs),
        ],
        compiler_params=pltpu.CompilerParams(collective_id=0, has_side_effects=True),
    )(block_len, target, queries, keys, values, cotangent, out_weight)
    if not finish:
        lines = [[i for i in range(n_dp) if i % group == g] for g in range(group)]
        grad = lax.psum(grad, "dp", axis_index_groups=lines)
        squares = lax.psum(jnp.sum(grad * grad), "fsdp")
        grad = grad * jnp.minimum(1.0, float(width) / jnp.sqrt(squares + 1e-06))
    return embedding, grad


def solution(mesh):
    n_dp, n_fs = mesh.shape["dp"], mesh.shape["fsdp"]
    group = math.gcd(n_dp, 4)
    both = P(("dp", "fsdp"), None, None)
    flat = P(("dp", "fsdp"))
    return jax.shard_map(
        functools.partial(local, n_dp, n_fs, group),
        mesh=mesh,
        in_specs=(both, both, both, flat, flat, both, P("fsdp", None)),
        out_specs=(both, P("fsdp", None)),
        check_vma=False,
    )
```

time: 202 us -> 68.4 us (0.34)
  waiting for transfers between devices: 127 us -> 0 us
  Pallas kernels: 0 us -> 62.7 us
  blocking collectives: 40 us -> 0 us
  between operations: 14.8 us -> 0.64 us
  matrix products: 11.3 us -> 0 us
  other arithmetic: 3.32 us -> 0 us
    reduce_scatter x1 -> x0, waiting for transfers between devices: 77.8 us -> none  [local(): lax.psum_scatter(lax.dot_general(columns, cot_rows, (((0,), (0,)), ((), (...]
    pallas_call x0 -> x1, Pallas kernels: none -> 62.7 us  [local(): pl.pallas_call(functools.partial(kernel, n_dp, n_fs, group, finish), out_...]
    all_gather x1 -> x0, waiting for transfers between devices: 41.6 us -> none  [local(): lax.all_gather(out_weight, 'fsdp', axis=0, tiled=True)]
    psum x2 -> x0, blocking collectives: 40 us -> none  [the longest x1 20.2 us: local(): summed = lax.psum(fsdp_summed, 'dp')]
    dot_general x4 -> x0, matrix products: 8.98 us -> none  [the longest x1 3.26 us: local(): jnp.dot(columns, lax.all_gather(out_weight, 'fsdp', axis=0, tiled=True),...]
    ppermute x1 -> x0, waiting for transfers between devices: 6.68 us -> none  [from_behind(): lax.ppermute(shard, axis, [(i, (i + by) % size) for i in range(size)])]
    sub x1 -> x0, matrix products: 2.34 us -> none  [attend(): exponent = jnp.exp(scores - highest)]
  transfers between devices with their start and end apart: 3 -> 0, of which waited for: 3 -> 0; matrix products, arithmetic and copies ran while one was open for 0% -> 0% of each run, Pallas kernels for 0% -> 0%
where the time goes in v1:
time: 68.4 us; the launch traced here: 67.1 us
  Pallas kernels  62.7 us (92%)
  local copies, waits for them, and re-layouts  3.81 us (6%)
    pallas_call x1, Pallas kernels, local(): pl.pallas_call(functools.partial(kernel, n_dp, n_fs, group, finish), out_...  62.7 us
    unnamed x2, local copies, waits for them, and re-layouts  3.81 us

profile of v1, /device:TPU:0, one launch (start us, length us, event | category | flops | bytes accessed | tf_op | source)
XLA Modules:
  0.0 67.1 jit_solution(1663557357237485615)
XLA Ops:
  0.6 62.7 %shard_map.86 = (bf16[1,128,1280]{2,1,0:T(8,128)(2,1)}, f32[160,1280]{1,0:T(8,128)}) custom-call(s32[2]{0:T(128)} %len_ref.1, s32[2]{0:T(128)} %tgt_ref.1, bf16[2,128,1280]{2,1,0:T(8,128)(2,1)} %q_ref.1, bf16[2,128,1280]{2,1,0:T(8,128)(2,1)} %k_ref.1, bf16[2,128,1280]{2,1,0:T(8,128)(2,1)} %v_ref.1, bf16[1,128,1280]{2,1,0:T(8,128)(2,1)} %cot_ref.1, ...), custom_call_target="tpu_custom_call" | custom-call | tf_op jit(solution)/shard_map/pallas_call | solution.py:256
  63.3 1.7 %copy.11 = bf16[1,128,1280]{2,1,0:T(8,128)(2,1)} copy(bf16[1,128,1280]{2,1,0:T(8,128)(2,1)} %get-tuple-element.4) | data formatting | bytes 655360
  65.0 2.1 %copy.12 = f32[160,1280]{1,0:T(8,128)} copy(f32[160,1280]{1,0:T(8,128)} %get-tuple-element.5) | data formatting | bytes 1638400

commit v2 on v1

--- a/solution.py
+++ b/solution.py
@@ -25,9 +25,9 @@
     n_dp, n_fs, group, finish,
     len_ref, tgt_ref, q_ref, k_ref, v_ref, cot_ref, w_ref,
     emb_ref, grad_ref,
-    wq, cq, mine, nxt, arr, placed, gpart, yrecv, zsend, zrecv, esend, ebuf, tbuf, sbuf, srecv,
+    wq, cq, mine, nxt, arr, placed, gpart, yrecv, zsend, zrecv, esend, ebuf, tbuf, sbuf, srecv, gsum,
     wz_s, wz_r, wy_s, wy_r, c_s, c_r, n_s, n_r, p_s, p_r, gy_s, gy_r, gz_s, gz_r,
-    e_s, e_r, t_s, t_r, q_s, q_r,
+    e_s, e_r, t_s, t_r, q_s, q_r, m_s, m_r,
 ):
     slots, rows, width = q_ref.shape
     shard = w_ref.shape[0]
@@ -42,6 +42,8 @@
     other = z * 2 + (1 - y)
     ahead, behind = (d + 1) % n_dp, (d + n_dp - 1) % n_dp
     mates = [(gi + j) % group for j in range(1, group)]
+    core, side = gi % 2, gi // 2
+    partner, across = side * 2 + (1 - core), (1 - side) * 2 + core
 
     def start_of(i):
         if group == 1:
@@ -52,6 +54,22 @@
         return pltpu.make_async_remote_copy(
             src_ref=src, dst_ref=dst, send_sem=s, recv_sem=r, device_id=to, device_id_type=MESH
         )
+
+    def spread(at, s, r):
+        to = [partner, across] if group == 4 else mates
+        made = [copy(at(gi), at(gi), s(j), r(j), (base + m, f)) for j, m in enumerate(to)]
+        for c in made:
+            c.start()
+        return made
+
+    def relay(made, at, s, r):
+        if group != 4:
+            return made
+        made[1].wait_recv()
+        c = copy(at(across), at(across), s(2), r(2), (base + partner, f))
+        c.start()
+        made.append(c)
+        return [made[0], c]
 
     barrier = pltpu.get_barrier_semaphore()
     peers = [(ahead, f), (behind, f)]
@@ -102,6 +120,21 @@
         c = copy(nxt.at[:, cols], arr.at[:, cols], n_s.at[part], n_r.at[part], (ahead, f))
         c.start()
         nexts.append(c)
+
+    def placed_at(part):
+        cols = pl.ds(part * half, half)
+        return lambda i: placed.at[pl.ds(pl.multiple_of(i * rows, rows), rows), cols]
+
+    def cast(part):
+        nexts[part].wait_recv()
+        cols = pl.ds(part * half, half)
+        placed[my_rows, cols] = mine[:, cols] + arr[:, cols]
+        return spread(placed_at(part), lambda j: p_s.at[part, j], lambda j: p_r.at[part, j])
+
+    def hand_on(part, made):
+        return relay(
+            made, placed_at(part), lambda j: p_s.at[part, j], lambda j: p_r.at[part, j]
+        )
 
     for h in range(HEADS):
         first, last = h * hd, (h + 1) * hd
@@ -131,7 +164,11 @@
                     ref[:, cols] = total.astype(BF16)
         if last == half:
             send_next(0)
+        if h == HEADS * 3 // 4 - 1:
+            cast0 = cast(0)
     send_next(1)
+    waits = hand_on(0, cast0)
+    cast1 = cast(1)
 
     for j in range(1, nz):
         wz[j - 1].wait_recv()
@@ -140,19 +177,9 @@
         c.start()
         wy.append(c)
 
-    casts = []
-    for part in range(2):
-        nexts[part].wait_recv()
-        cols = pl.ds(part * half, half)
-        placed[my_rows, cols] = mine[:, cols] + arr[:, cols]
-        for j, m in enumerate(mates):
-            c = copy(
-                placed.at[my_rows, cols], placed.at[my_rows, cols],
-                p_s.at[part, j], p_r.at[part, j], (base + m, f),
-            )
-            c.start()
-            casts.append(c)
-    for c in cots + casts:
+    waits += hand_on(1, cast1)
+    casts = cast0 + cast1
+    for c in cots + waits:
         c.wait_recv()
 
     step = 2 * LANES
@@ -205,35 +232,49 @@
         c.wait_recv()
     for j in range(1, nz):
         own = own + zrecv[j].astype(F32)
+    ends = starts[1:] + [width]
     tbuf[gi] = own.astype(BF16)
-    turns = []
-    for j, m in enumerate(mates):
-        c = copy(tbuf.at[gi], tbuf.at[gi], t_s.at[j], t_r.at[j], (base + m, f))
-        c.start()
-        turns.append(c)
-    for c in embs:
-        c.wait_recv()
-    ends = starts[1:] + [width]
-    for i in range(group):
-        emb_ref[0, :, starts[i]:ends[i]] = ebuf[i, :, 0:ends[i] - starts[i]]
-    for c in turns:
-        c.wait_recv()
+    turn_at = lambda i: tbuf.at[i]
+    turn_s, turn_r = (lambda j: t_s.at[j]), (lambda j: t_r.at[j])
+    turns = spread(turn_at, turn_s, turn_r)
     squares = []
     if finish:
+        valid = window
+        for i in range(group):
+            valid = jnp.where(gi == i, ends[i] - starts[i], valid)
+        lane = lax.broadcasted_iota(jnp.int32, (8, LANES), 1)
         total = jnp.zeros((8, LANES), F32)
-        for i in range(group):
-            for col in range(0, ends[i] - starts[i], LANES):
-                tile = tbuf[i, :, col:col + LANES].astype(F32)
-                total = total + jnp.sum((tile * tile).reshape(shard // 8, 8, LANES), axis=0)
+        for col in range(0, window, LANES):
+            tile = own[:, col:col + LANES].astype(BF16).astype(F32)
+            part = jnp.sum((tile * tile).reshape(shard // 8, 8, LANES), axis=0)
+            total = total + jnp.where(lane + col < valid, part, 0.0)
         sbuf[...] = total
         for j in range(1, n_fs):
             c = copy(sbuf, srecv.at[j], q_s.at[j], q_r.at[j], (d, (f + j) % n_fs))
             c.start()
             squares.append(c)
-        for c in squares:
+    waits = relay(turns, turn_at, turn_s, turn_r)
+    if finish:
+        for j, c in zip(range(1, n_fs), squares):
             c.wait_recv()
-        for j in range(1, n_fs):
             total = total + srecv[j]
+        gsum[gi] = total
+        for j, m in enumerate(mates):
+            c = copy(gsum.at[gi], gsum.at[gi], m_s.at[j], m_r.at[j], (base + m, f))
+            c.start()
+            squares.append(c)
+    for c in embs:
+        c.wait_recv()
+    for i in range(group):
+        emb_ref[0, :, starts[i]:ends[i]] = ebuf[i, :, 0:ends[i] - starts[i]]
+    for c in waits:
+        c.wait_recv()
+    if finish:
+        for c in squares[n_fs - 1:]:
+            c.wait_recv()
+        total = gsum[0]
+        for i in range(1, group):
+            total = total + gsum[i]
         norm = jnp.sqrt(jnp.sum(total, keepdims=True) + 1e-06)
         factor = jnp.minimum(1.0, float(width) / norm)
     for i in range(group):
@@ -277,9 +318,11 @@
             pltpu.VMEM((group, shard, window), BF16),
             pltpu.VMEM((8, LANES), F32),
             pltpu.VMEM((n_fs, 8, LANES), F32),
+            pltpu.VMEM((group, 8, LANES), F32),
             sem(nz), sem(nz), sem(nz), sem(nz), sem(mates), sem(mates), sem(2), sem(2),
             sem(2, mates), sem(2, mates), sem(nz), sem(nz), sem(nz), sem(nz),
             sem(mates), sem(mates), sem(mates), sem(mates), sem(n_fs), sem(n_fs),
+            sem(mates), sem(mates),
         ],
         compiler_params=pltpu.CompilerParams(collective_id=0, has_side_effects=True),
     )(block_len, target, queries, keys, values, cotangent, out_weight)

time: 68.4 us -> 57.3 us (0.84); the launches traced: 67.1 us -> 57.1 us
  Pallas kernels: 62.7 us -> 52.7 us
    pallas_call x1, Pallas kernels: 62.7 us -> 52.7 us  [local(): pl.pallas_call(functools.partial(kernel, n_dp, n_fs, group, finish), out_...]
where the time goes in v2:
time: 57.3 us; the launch traced here: 57.1 us
  Pallas kernels  52.7 us (92%)
  local copies, waits for them, and re-layouts  3.81 us (7%)
  between operations  0.64 us (1%)
    pallas_call x1, Pallas kernels, local(): pl.pallas_call(functools.partial(kernel, n_dp, n_fs, group, finish), out_...  52.7 us
    unnamed x2, local copies, waits for them, and re-layouts  3.81 us

profile of v2, /device:TPU:0, one launch (start us, length us, event | category | flops | bytes accessed | tf_op | source)
XLA Modules:
  0.0 57.1 jit_solution(5213021607586095661)
XLA Ops:
  0.6 52.7 %shard_map.86 = (bf16[1,128,1280]{2,1,0:T(8,128)(2,1)}, f32[160,1280]{1,0:T(8,128)}) custom-call(s32[2]{0:T(128)} %len_ref.1, s32[2]{0:T(128)} %tgt_ref.1, bf16[2,128,1280]{2,1,0:T(8,128)(2,1)} %q_ref.1, bf16[2,128,1280]{2,1,0:T(8,128)(2,1)} %k_ref.1, bf16[2,128,1280]{2,1,0:T(8,128)(2,1)} %v_ref.1, bf16[1,128,1280]{2,1,0:T(8,128)(2,1)} %cot_ref.1, ...), custom_call_target="tpu_custom_call" | custom-call | tf_op jit(solution)/shard_map/pallas_call | solution.py:297
  53.3 1.7 %copy.11 = bf16[1,128,1280]{2,1,0:T(8,128)(2,1)} copy(bf16[1,128,1280]{2,1,0:T(8,128)(2,1)} %get-tuple-element.4) | data formatting | bytes 655360
  55.0 2.1 %copy.12 = f32[160,1280]{1,0:T(8,128)} copy(f32[160,1280]{1,0:T(8,128)} %get-tuple-element.5) | data formatting | bytes 1638400

commit v3 on v2

--- a/solution.py
+++ b/solution.py
@@ -21,10 +21,15 @@
     return window, [min(i * window, width - window) for i in range(group)]
 
 
+def marks_of(width):
+    tiles = width // LANES
+    return [tiles * tenths // 10 * LANES for tenths in (0, 4, 7, 9, 10)]
+
+
 def kernel(
     n_dp, n_fs, group, finish,
     len_ref, tgt_ref, q_ref, k_ref, v_ref, cot_ref, w_ref,
-    emb_ref, grad_ref,
+    emb_ref, grad_ref, factor_ref,
     wq, cq, mine, nxt, arr, placed, gpart, yrecv, zsend, zrecv, esend, ebuf, tbuf, sbuf, srecv, gsum,
     wz_s, wz_r, wy_s, wy_r, c_s, c_r, n_s, n_r, p_s, p_r, gy_s, gy_r, gz_s, gz_r,
     e_s, e_r, t_s, t_r, q_s, q_r, m_s, m_r,
@@ -77,7 +82,6 @@
     peers += [(d, (f + j) % n_fs) for j in range(1, n_fs)]
     for peer in peers:
         pl.semaphore_signal(barrier, inc=1, device_id=peer, device_id_type=MESH)
-    pl.semaphore_wait(barrier, len(peers))
 
     my_cols = pl.ds(start_of(gi), window)
     my_rows = pl.ds(pl.multiple_of(gi * rows, rows), rows)
@@ -85,25 +89,26 @@
     def w_at(index):
         return wq.at[pl.ds(pl.multiple_of(index * shard, shard), shard), :]
 
-    sends = []
-    w_src = w_ref.at[:, my_cols]
-    wz = []
-    for j in range(1, nz):
-        c = copy(w_src, w_at(f), wz_s.at[j], wz_r.at[j], (d, ((z + j) % nz) * 2 + y))
-        c.start()
-        wz.append(c)
-    wy = [copy(w_src, w_at(f), wy_s.at[0], wy_r.at[0], (d, other))]
-    wy[0].start()
-    cots = []
-    for j, m in enumerate(mates):
-        c = copy(
-            cot_ref.at[0, :, pl.ds(start_of(m), window)], cq.at[my_rows, :],
-            c_s.at[j], c_r.at[j], (base + m, f),
-        )
-        c.start()
-        cots.append(c)
-    wq[pl.ds(pl.multiple_of(f * shard, shard), shard), :] = w_ref[:, my_cols]
-    cq[my_rows, :] = cot_ref[0, :, my_cols]
+    wz, wy, cots = [], [], []
+
+    def open_links():
+        pl.semaphore_wait(barrier, len(peers))
+        w_src = w_ref.at[:, my_cols]
+        for j in range(1, nz):
+            c = copy(w_src, w_at(f), wz_s.at[j], wz_r.at[j], (d, ((z + j) % nz) * 2 + y))
+            c.start()
+            wz.append(c)
+        wy.append(copy(w_src, w_at(f), wy_s.at[0], wy_r.at[0], (d, other)))
+        wy[0].start()
+        for j, m in enumerate(mates):
+            c = copy(
+                cot_ref.at[0, :, pl.ds(start_of(m), window)], cq.at[my_rows, :],
+                c_s.at[j], c_r.at[j], (base + m, f),
+            )
+            c.start()
+            cots.append(c)
+        wq[pl.ds(pl.multiple_of(f * shard, shard), shard), :] = w_ref[:, my_cols]
+        cq[my_rows, :] = cot_ref[0, :, my_cols]
 
     key_pos = lax.broadcasted_iota(jnp.int32, (rows, rows), 1)
     row_pos = lax.broadcasted_iota(jnp.int32, (rows, LANES), 0)
@@ -112,22 +117,23 @@
     limit = [[jnp.where(tgt_ref[s] == t, lens[s], 0) for s in range(slots)] for t in range(2)]
     keep = [[row_pos < limit[t][s] for s in range(slots)] for t in range(2)]
     tiles = {}
-    half = width // 2
-    nexts = []
+    marks = marks_of(width)
+    parts = len(marks) - 1
+    nexts, cast_all = [], []
 
     def send_next(part):
-        cols = pl.ds(part * half, half)
+        cols = pl.ds(marks[part], marks[part + 1] - marks[part])
         c = copy(nxt.at[:, cols], arr.at[:, cols], n_s.at[part], n_r.at[part], (ahead, f))
         c.start()
         nexts.append(c)
 
     def placed_at(part):
-        cols = pl.ds(part * half, half)
+        cols = pl.ds(marks[part], marks[part + 1] - marks[part])
         return lambda i: placed.at[pl.ds(pl.multiple_of(i * rows, rows), rows), cols]
 
     def cast(part):
         nexts[part].wait_recv()
-        cols = pl.ds(part * half, half)
+        cols = pl.ds(marks[part], marks[part + 1] - marks[part])
         placed[my_rows, cols] = mine[:, cols] + arr[:, cols]
         return spread(placed_at(part), lambda j: p_s.at[part, j], lambda j: p_r.at[part, j])
 
@@ -162,14 +168,17 @@
                         jnp.where(keep[dest][s], tiles[s, t], 0.0) for s in range(slots)
                     )
                     ref[:, cols] = total.astype(BF16)
-        if last == half:
-            send_next(0)
-        if h == HEADS * 3 // 4 - 1:
-            cast0 = cast(0)
-    send_next(1)
-    waits = hand_on(0, cast0)
-    cast1 = cast(1)
-
+        if h == HEADS // 8 - 1:
+            open_links()
+        ready = last // LANES * LANES
+        while len(nexts) < parts - 1 and marks[len(nexts) + 1] <= ready:
+            send_next(len(nexts))
+            if len(nexts) > 1:
+                cast_all.append(cast(len(nexts) - 2))
+    send_next(parts - 1)
+    cast_all.append(cast(parts - 2))
+    waits = hand_on(0, cast_all[0])
+    cast_all.append(cast(parts - 1))
     for j in range(1, nz):
         wz[j - 1].wait_recv()
         from_f = ((z + nz - j) % nz) * 2 + y
@@ -177,8 +186,9 @@
         c.start()
         wy.append(c)
 
-    waits += hand_on(1, cast1)
-    casts = cast0 + cast1
+    for part in range(1, parts):
+        waits += hand_on(part, cast_all[part])
+    casts = sum(cast_all, [])
     for c in cots + waits:
         c.wait_recv()
 
@@ -278,10 +288,15 @@
         norm = jnp.sqrt(jnp.sum(total, keepdims=True) + 1e-06)
         factor = jnp.minimum(1.0, float(width) / norm)
     for i in range(group):
-        tile = tbuf[i, :, 0:ends[i] - starts[i]].astype(F32)
-        grad_ref[:, starts[i]:ends[i]] = tile * factor if finish else tile
+        grad_ref[:, starts[i]:ends[i]] = tbuf[i, :, 0:ends[i] - starts[i]]
+    factor_ref[...] = jnp.broadcast_to(factor, factor_ref.shape) if finish else jnp.ones_like(factor_ref)
     for c in wz + wy + cots + nexts + casts + gy + gz + embs + turns + squares:
         c.wait_send()
+
+
+def settle(emb_ref, rows_ref, factor_ref, emb_out, grad_out):
+    emb_out[...] = emb_ref[...]
+    grad_out[...] = rows_ref[...].astype(F32) * factor_ref[0:1, 0:1]
 
 
 def local(n_dp, n_fs, group, queries, keys, values, block_len, target, cotangent, out_weight):
@@ -294,14 +309,16 @@
     smem = pl.BlockSpec(memory_space=pltpu.SMEM)
     sem = lambda *shape: pltpu.SemaphoreType.DMA(shape)
     mates = max(group - 1, 1)
-    embedding, grad = pl.pallas_call(
+    parts = len(marks_of(width)) - 1
+    embedding, rows_sum, factor = pl.pallas_call(
         functools.partial(kernel, n_dp, n_fs, group, finish),
         out_shape=(
             jax.ShapeDtypeStruct(cotangent.shape, BF16),
-            jax.ShapeDtypeStruct((shard, width), F32),
+            jax.ShapeDtypeStruct((shard, width), BF16),
+            jax.ShapeDtypeStruct((8, LANES), F32),
         ),
         in_specs=[smem, smem] + [vmem] * 5,
-        out_specs=(vmem, vmem),
+        out_specs=(vmem, vmem, vmem),
         scratch_shapes=[
             pltpu.VMEM((width, window), BF16),
             pltpu.VMEM((group * rows, window), BF16),
@@ -319,13 +336,22 @@
             pltpu.VMEM((8, LANES), F32),
             pltpu.VMEM((n_fs, 8, LANES), F32),
             pltpu.VMEM((group, 8, LANES), F32),
-            sem(nz), sem(nz), sem(nz), sem(nz), sem(mates), sem(mates), sem(2), sem(2),
-            sem(2, mates), sem(2, mates), sem(nz), sem(nz), sem(nz), sem(nz),
+            sem(nz), sem(nz), sem(nz), sem(nz), sem(mates), sem(mates), sem(parts), sem(parts),
+            sem(parts, mates), sem(parts, mates), sem(nz), sem(nz), sem(nz), sem(nz),
             sem(mates), sem(mates), sem(mates), sem(mates), sem(n_fs), sem(n_fs),
             sem(mates), sem(mates),
         ],
         compiler_params=pltpu.CompilerParams(collective_id=0, has_side_effects=True),
     )(block_len, target, queries, keys, values, cotangent, out_weight)
+    embedding, grad = pl.pallas_call(
+        settle,
+        out_shape=(
+            jax.ShapeDtypeStruct(cotangent.shape, BF16),
+            jax.ShapeDtypeStruct((shard, width), F32),
+        ),
+        in_specs=[vmem] * 3,
+        out_specs=(vmem, vmem),
+    )(embedding, rows_sum, factor)
     if not finish:
         lines = [[i for i in range(n_dp) if i % group == g] for g in range(group)]
         grad = lax.psum(grad, "dp", axis_index_groups=lines)

time: 57.3 us -> 55.8 us (0.974)
  local copies, waits for them, and re-layouts: 3.81 us -> 0 us
  Pallas kernels: 52.7 us -> 55 us
    unnamed x2 -> x0, local copies, waits for them, and re-layouts: 3.81 us -> none
    pallas_call x0 -> x1, Pallas kernels: none -> 2.12 us  [local(): pl.pallas_call(settle, out_shape=(jax.ShapeDtypeStruct(cotangent.shape, B...]
where the time goes in v3:
time: 55.8 us; the launch traced here: 55.7 us
  Pallas kernels  55 us (99%)
  between operations  0.64 us (1%)
    pallas_call x1, Pallas kernels, local(): pl.pallas_call(functools.partial(kernel, n_dp, n_fs, group, finish), out_...  52.9 us
    pallas_call x1, Pallas kernels, local(): pl.pallas_call(settle, out_shape=(jax.ShapeDtypeStruct(cotangent.shape, B...  2.12 us

profile of v3, /device:TPU:0, one launch (start us, length us, event | category | flops | bytes accessed | tf_op | source)
XLA Modules:
  0.0 55.7 jit_solution(18271039118112699943)
XLA Ops:
  0.6 52.9 %shard_map.86 = (bf16[1,128,1280]{2,1,0:T(8,128)(2,1)}, bf16[160,1280]{1,0:T(8,128)(2,1)}, f32[8,128]{1,0:T(8,128)}) custom-call(s32[2]{0:T(128)} %len_ref.1, s32[2]{0:T(128)} %tgt_ref.1, bf16[2,128,1280]{2,1,0:T(8,128)(2,1)} %q_ref.1, bf16[2,128,1280]{2,1,0:T(8,128)(2,1)} %k_ref.1, bf16[2,128,1280]{2,1,0:T(8,128)(2,1)} %v_ref.1, ...), custom_call_target="tpu_custom_call" | custom-call | tf_op jit(solution)/shard_map/pallas_call | solution.py:313
  53.5 2.1 %shard_map.87 = (bf16[1,128,1280]{2,1,0:T(8,128)(2,1)}, f32[160,1280]{1,0:T(8,128)}) custom-call(bf16[1,128,1280]{2,1,0:T(8,128)(2,1)} %get-tuple-element.5.emb_ref, bf16[160,1280]{1,0:T(8,128)(2,1)} %get-tuple-element.6.rows_ref, f32[8,128]{1,0:T(8,128)} %get-tuple-element.7.factor_ref), custom_call_target="tpu_custom_call" | custom-call | tf_op jit(solution)/shard_map/pallas_call | solution.py:346

commit v4 on v3

--- a/solution.py
+++ b/solution.py
@@ -202,7 +202,7 @@
     def g_rows(index):
         return pl.ds(pl.multiple_of(index * shard, shard), shard)
 
-    order = list(range(1, nz)) + [0]
+    order = sorted(range(1, nz), key=lambda j: abs(2 * j - nz)) + [0]
     gy = []
     for j in order:
         zj = (z + j) % nz

time: 55.8 us -> 55.8 us (level)
  no operation moved by 1% of the time
where the time goes in v4:
time: 55.8 us; the launch traced here: 55.7 us
  Pallas kernels  55 us (99%)
  between operations  0.64 us (1%)
    pallas_call x1, Pallas kernels, local(): pl.pallas_call(functools.partial(kernel, n_dp, n_fs, group, finish), out_...  52.9 us
    pallas_call x1, Pallas kernels, local(): pl.pallas_call(settle, out_shape=(jax.ShapeDtypeStruct(cotangent.shape, B...  2.12 us

profile of v4, /device:TPU:0, one launch (start us, length us, event | category | flops | bytes accessed | tf_op | source)
XLA Modules:
  0.0 55.7 jit_solution(10940574838861986456)
XLA Ops:
  0.6 52.9 %shard_map.86 = (bf16[1,128,1280]{2,1,0:T(8,128)(2,1)}, bf16[160,1280]{1,0:T(8,128)(2,1)}, f32[8,128]{1,0:T(8,128)}) custom-call(s32[2]{0:T(128)} %len_ref.1, s32[2]{0:T(128)} %tgt_ref.1, bf16[2,128,1280]{2,1,0:T(8,128)(2,1)} %q_ref.1, bf16[2,128,1280]{2,1,0:T(8,128)(2,1)} %k_ref.1, bf16[2,128,1280]{2,1,0:T(8,128)(2,1)} %v_ref.1, ...), custom_call_target="tpu_custom_call" | custom-call | tf_op jit(solution)/shard_map/pallas_call | solution.py:313
  53.5 2.1 %shard_map.87 = (bf16[1,128,1280]{2,1,0:T(8,128)(2,1)}, f32[160,1280]{1,0:T(8,128)}) custom-call(bf16[1,128,1280]{2,1,0:T(8,128)(2,1)} %get-tuple-element.5.emb_ref, bf16[160,1280]{1,0:T(8,128)(2,1)} %get-tuple-element.6.rows_ref, f32[8,128]{1,0:T(8,128)} %get-tuple-element.7.factor_ref), custom_call_target="tpu_custom_call" | custom-call | tf_op jit(solution)/shard_map/pallas_call | solution.py:346
